TPU v7x, 32 devices: a whole 2x2x4 slice. The times are simulated.
32 devices in a mesh: groups: 2 (over y), ctx: 16 (over z, x, core).
Axes of the slice: x: 2, y: 2, z: 4, core: 2. Of those that a mesh axis runs over, the one named last changes fastest.
Arguments:
- queries: bfloat16 [512, 5120], P(('groups', 'ctx')), parts along dimension 0, may hold values from -45 to 45
- keys: bfloat16 [49152, 1024], P(('groups', 'ctx')), parts along dimension 0, may hold values from -5 to 5
- values: bfloat16 [49152, 1024], P(('groups', 'ctx')), parts along dimension 0, may hold values from -10 to 10
- block_mask: int32 [16, 2, 192], P('groups', None, 'ctx'), parts along dimension 0, may hold values from 0 to 1, as said below
- out_weight: bfloat16 [5120, 5120], P('ctx'), may hold values from -0.078125 to 0.078125
Outputs:
- projected: bfloat16 [512, 5120], P(('groups', 'ctx')), parts along dimension 0
There are 2 independent parts, one for each index of `groups`. A program takes and returns all parts, laid end to end along the dimension named above; an argument that names none is the same for every part. Nothing has to cross between parts.
Inputs may be any that keep to these rules, and one draw needn't show every extreme that they name: `block_mask`: for every key head and query block at least one key block is 1; the share of 1s differs between spans of 1536 positions.
All inputs are finite; a program needn't handle non-finite values.
Results may differ from a plain program's by a relative error of at most 0.0055.
Values may be sent and summed in bfloat16 or wider, within the bound.
A program may use at most 128 MiB of HBM per device.

v0:
```python
import functools
import math

import jax
import jax.numpy as jnp
from jax import lax
from jax.experimental import pallas as pl
from jax.experimental.pallas import tpu as pltpu
from jax.sharding import PartitionSpec as P

HEAD_SIZE = 128
NEG = -1e30
ONES = 16
LOG2E = math.log2(math.e)
MESH = pl.DeviceIdType.MESH
CORES, ROW = 2, 2


def attend_kernel(rows_each, mask_ref, q_ref, k_ref, v_ref, *refs):
    *numer_refs, top_ref, total_ref, live_ref, score_ref, query_ref, value_ref, sum_ref = refs
    head = pl.program_id(0)
    query_blocks, key_blocks = mask_ref.shape[1:]
    key_block = k_ref.shape[0] // key_blocks
    query_block = q_ref.shape[0] // query_blocks
    group = q_ref.shape[1] // HEAD_SIZE
    factor = LOG2E / math.sqrt(HEAD_SIZE)
    value_ref[:HEAD_SIZE] = v_ref[...].T
    value_ref[HEAD_SIZE:] = jnp.ones((ONES, v_ref.shape[0]), jnp.bfloat16)
    for at in range(query_blocks):
        rows = pl.ds(at * query_block, query_block)
        count = jnp.int32(0)
        for block in range(key_blocks):
            live_ref[count] = block
            count = count + (mask_ref[head, at, block] > 0).astype(jnp.int32)
        live_ref[count] = 0
        for g in range(group):
            tokens = q_ref[rows, g * HEAD_SIZE : (g + 1) * HEAD_SIZE]
            query_ref[:, g * query_block : (g + 1) * query_block] = tokens.T
        lanes = query_ref.shape[1]
        pairs = (count + 1) // 2

        def start_of(which):
            return pl.multiple_of(live_ref[which] * key_block, key_block)

        eights, quads = (count + 1) // 8, (count + 1) // 4

        def taken(ref_slice, first, blocks, axis):
            return jnp.concatenate([ref_slice(start_of(first + b)) for b in range(blocks)], axis=axis)

        def score_step(blocks, step, top):
            pair = step * (blocks // 2)
            keys = taken(lambda at: k_ref[pl.ds(at, key_block), :], 2 * pair, blocks, 0)
            scores = jnp.dot(keys, query_ref[...], preferred_element_type=jnp.float32)
            score_ref[pl.ds(pair, blocks // 2)] = scores.reshape(blocks // 2, 2 * key_block, lanes)
            tops = jnp.max(scores.reshape(blocks, key_block // 8, 8, lanes), axis=1)
            for b in range(blocks):
                one = tops[b]
                if b == blocks - 1:
                    one = jnp.where(2 * pair + b < count, one, NEG)
                top = jnp.maximum(top, one)
            return top

        top = jnp.full((8, lanes), NEG, jnp.float32)
        top = lax.fori_loop(0, eights, functools.partial(score_step, 8), top)
        top = lax.fori_loop(2 * eights, quads, functools.partial(score_step, 4), top)
        top = lax.fori_loop(2 * quads, pairs, functools.partial(score_step, 2), top)
        top = jnp.max(top, axis=0, keepdims=True) * factor
        sum_ref[...] = jnp.zeros_like(sum_ref)

        def sum_step(blocks, step, _):
            pair = step * (blocks // 2)
            probs = []
            for b in range(blocks):
                shift = top
                if b == blocks - 1:
                    shift = jnp.where(2 * pair + b < count, top, -NEG)
                half = slice(b % 2 * key_block, (b % 2 + 1) * key_block)
                scores = score_ref[pair + b // 2, half]
                probs.append(jnp.exp2(scores * factor - shift).astype(jnp.bfloat16))
            values = taken(lambda at: value_ref[:, pl.ds(at, key_block)], 2 * pair, blocks, 1)
            sum_ref[...] += jnp.dot(
                values, jnp.concatenate(probs, axis=0), preferred_element_type=jnp.float32
            )
            return 0

        lax.fori_loop(0, eights, functools.partial(sum_step, 8), 0)
        lax.fori_loop(2 * eights, quads, functools.partial(sum_step, 4), 0)
        lax.fori_loop(2 * quads, pairs, functools.partial(sum_step, 2), 0)
        numer = sum_ref[:HEAD_SIZE]
        top_ref[0, at : at + 1, :] = top
        total_ref[0, at : at + 1, :] = sum_ref[HEAD_SIZE : HEAD_SIZE + 1]
        for g in range(group):
            columns = slice(g * query_block, (g + 1) * query_block)
            out_columns = slice(g * HEAD_SIZE, (g + 1) * HEAD_SIZE)
            tokens = numer[:, columns].T
            if not rows_each:
                numer_refs[0][rows, out_columns] = tokens
                continue
            tokens = tokens.reshape(-1, CORES, rows_each, HEAD_SIZE)
            first = lax.rem(lax.axis_index("ctx"), CORES) == 0
            half = pl.ds(at * query_block // CORES, query_block // CORES)
            kept = jnp.where(first, tokens[:, 0], tokens[:, 1]).reshape(-1, HEAD_SIZE)
            sent = jnp.where(first, tokens[:, 1], tokens[:, 0]).reshape(-1, HEAD_SIZE)
            numer_refs[0][half, out_columns] = kept
            numer_refs[1][half, out_columns] = sent.astype(jnp.bfloat16)


def attend(whole, keys, values, block_mask, rows_each):
    qtok, width = whole.shape
    kdev = keys.shape[0]
    heads_kv, query_blocks, key_blocks = block_mask.shape
    columns = width // heads_kv
    lanes = columns // HEAD_SIZE * (qtok // query_blocks)
    stat = jax.ShapeDtypeStruct((heads_kv, query_blocks, lanes), jnp.float32)
    stat_spec = pl.BlockSpec((1, query_blocks, lanes), lambda h: (h, 0, 0))
    numers = [jax.ShapeDtypeStruct((qtok, width), jnp.float32)]
    if rows_each:
        numers = [jax.ShapeDtypeStruct((qtok // CORES, width), t) for t in (jnp.float32, jnp.bfloat16)]
    return pl.pallas_call(
        functools.partial(attend_kernel, rows_each),
        grid=(heads_kv,),
        out_shape=(*numers, stat, stat),
        in_specs=[
            pl.BlockSpec(memory_space=pltpu.SMEM),
            pl.BlockSpec((qtok, columns), lambda h: (0, h)),
            pl.BlockSpec((kdev, HEAD_SIZE), lambda h: (0, h)),
            pl.BlockSpec((kdev, HEAD_SIZE), lambda h: (0, h)),
        ],
        out_specs=(
            *(pl.BlockSpec((numer.shape[0], columns), lambda h: (0, h)) for numer in numers),
            stat_spec,
            stat_spec,
        ),
        scratch_shapes=[
            pltpu.SMEM((key_blocks + 2,), jnp.int32),
            pltpu.VMEM(((key_blocks + 1) // 2, 2 * kdev // key_blocks, lanes), jnp.float32),
            pltpu.VMEM((HEAD_SIZE, lanes), jnp.bfloat16),
            pltpu.VMEM((HEAD_SIZE + ONES, kdev), jnp.bfloat16),
            pltpu.VMEM((HEAD_SIZE + ONES, lanes), jnp.float32),
        ],
        compiler_params=pltpu.CompilerParams(vmem_limit_bytes=60 * 2**20),
        name="attend",
    )(block_mask, whole, keys, values)


def by_token(stat, qtok):
    heads_kv, query_blocks, _ = stat.shape
    stat = stat.reshape(heads_kv, query_blocks, -1, qtok // query_blocks)
    return stat.transpose(1, 3, 0, 2).reshape(qtok, -1)


def shards_any(queries, keys, values, block_mask, out_weight):
    whole = lax.all_gather(queries, "ctx", axis=0, tiled=True)
    qtok, width = whole.shape
    numer, top, total = attend(whole, keys, values, block_mask, 0)
    rescale = by_token(jnp.exp2(top - lax.pmax(top, "ctx")), qtok)
    denom = by_token(total, qtok) * rescale
    numer = (numer.reshape(qtok, -1, HEAD_SIZE) * rescale[:, :, None]).reshape(qtok, width)
    num_rows = lax.psum_scatter(numer, "ctx", scatter_dimension=0, tiled=True)
    den_rows = lax.psum_scatter(denom, "ctx", scatter_dimension=0, tiled=True)
    own_rows = num_rows.shape[0]
    attn_rows = (num_rows.reshape(own_rows, -1, HEAD_SIZE) / den_rows[:, :, None]).reshape(
        own_rows, width
    )
    attn_cols = lax.all_to_all(
        attn_rows.astype(jnp.bfloat16), "ctx", split_axis=1, concat_axis=0, tiled=True
    )
    summed = lax.psum_scatter(
        jnp.dot(attn_cols, out_weight, preferred_element_type=jnp.float32),
        "ctx",
        scatter_dimension=0,
        tiled=True,
    )
    return summed.astype(jnp.bfloat16)


def place(n):
    me = lax.axis_index("ctx")
    core = lax.rem(me, CORES)
    x = lax.rem(me // CORES, ROW)
    plane = me // (CORES * ROW)
    return me, plane, x, core


def index_of(plane, x, core):
    return (plane * ROW + x) * CORES + core


def greet(devices):
    barrier = pltpu.get_barrier_semaphore()
    for device in devices:
        pl.semaphore_signal(barrier, inc=1, device_id={"ctx": device}, device_id_type=MESH)
    pl.semaphore_wait(barrier, len(devices))


def remote(src, dst, send, recv, device):
    return pltpu.make_async_remote_copy(
        src_ref=src,
        dst_ref=dst,
        send_sem=send,
        recv_sem=recv,
        device_id={"ctx": device},
        device_id_type=MESH,
    )


def gather_kernel(n, own_ref, whole_ref, own_sem, send_sem, recv_sem):
    me, plane, x, core = place(n)
    planes = n // (CORES * ROW)
    beside, sibling = 1 - x, 1 - core
    barrier = pltpu.get_barrier_semaphore()

    def hello(device):
        pl.semaphore_signal(barrier, inc=1, device_id={"ctx": device}, device_id_type=MESH)

    hello(index_of(plane, beside, core))
    hello(index_of(plane, x, sibling))

    @pl.when(plane > 0)
    def _():
        hello(index_of(plane - 1, x, core))

    @pl.when(plane < planes - 1)
    def _():
        hello(index_of(plane + 1, x, core))

    ends = (plane > 0).astype(jnp.int32) + (plane < planes - 1).astype(jnp.int32)
    pl.semaphore_wait(barrier, 2 + ends)
    own = pltpu.make_async_copy(own_ref, whole_ref.at[me], own_sem)
    own.start()

    def copy_to(block, way, device, mine=False):
        src = own_ref if mine else whole_ref.at[block]
        return remote(src, whole_ref.at[block], send_sem.at[way, block], recv_sem.at[block], device)

    def arrived(block):
        copy_to(block, 0, me).wait_recv()

    def pass_on(p, up, act, mine=False):
        block = index_of(p, x, core)

        @pl.when(plane + up < planes if up > 0 else plane + up >= 0)
        def _():
            act(copy_to(block, 0 if up > 0 else 1, index_of(plane + up, x, core), mine))

    start, ended = (lambda copy: copy.start()), (lambda copy: copy.wait_send())
    pass_on(plane, 1, start, True)
    pass_on(plane, -1, start, True)
    copy_to(me, 2, index_of(plane, beside, core), True).start()
    copy_to(me, 3, index_of(plane, x, sibling), True).start()
    for distance in range(1, planes):
        for up in (1, -1):
            p = plane - up * distance

            @pl.when(p >= 0 if up > 0 else p < planes)
            def _():
                block = index_of(p, x, core)
                arrived(block)
                pass_on(p, up, start)
                copy_to(block, 2, index_of(plane, beside, core)).start()
                copy_to(block, 3, index_of(plane, x, sibling)).start()

    def near_first(act):
        act(plane)
        for distance in range(1, planes):
            for up in (1, -1):
                p = plane - up * distance

                @pl.when(p >= 0 if up > 0 else p < planes)
                def _():
                    act(p)

    def from_beside(p):
        block = index_of(p, beside, core)
        arrived(block)
        copy_to(block, 3, index_of(plane, x, sibling)).start()

    def from_sibling(p):
        arrived(index_of(p, x, sibling))
        arrived(index_of(p, beside, sibling))

    near_first(from_beside)
    near_first(from_sibling)
    pass_on(plane, 1, ended, True)
    pass_on(plane, -1, ended, True)
    for distance in range(1, planes):
        for up in (1, -1):
            p = plane - up * distance

            @pl.when(p >= 0 if up > 0 else p < planes)
            def _():
                pass_on(p, up, ended)

    def sent(p):
        copy_to(index_of(p, x, core), 2, index_of(plane, beside, core)).wait_send()
        copy_to(index_of(p, x, core), 3, index_of(plane, x, sibling)).wait_send()
        copy_to(index_of(p, beside, core), 3, index_of(plane, x, sibling)).wait_send()

    near_first(sent)
    own.wait()


def gather_rows(queries, n):
    rows, width = queries.shape
    whole = pl.pallas_call(
        functools.partial(gather_kernel, n),
        out_shape=jax.ShapeDtypeStruct((n, rows, width), queries.dtype),
        in_specs=[pl.BlockSpec(memory_space=pltpu.VMEM)],
        out_specs=pl.BlockSpec(memory_space=pltpu.VMEM),
        scratch_shapes=[
            pltpu.SemaphoreType.DMA,
            pltpu.SemaphoreType.DMA((4, n)),
            pltpu.SemaphoreType.DMA((n,)),
        ],
        compiler_params=pltpu.CompilerParams(collective_id=0, has_side_effects=True),
        name="gather_rows",
    )(queries)
    return whole.reshape(n * rows, width)


def reduce_rows(place_of, parts, merge, finish):
    plane, x, core, planes = place_of
    beside, sibling = 1 - x, 1 - core
    others = [lax.rem(plane + step, planes) for step in range(1, planes)]

    def turn(step):
        return lax.rem(plane + 1 + step, planes)

    def core_copy(part, p):
        sem = part[9]
        return remote(
            part[0](p), part[2].at[p], sem.at[0, p], sem.at[1, p], index_of(plane, x, sibling)
        )

    def beside_copy(part, p):
        sem = part[9]
        return remote(
            part[3].at[p], part[5].at[p], sem.at[2, p], sem.at[3, p], index_of(plane, beside, core)
        )

    def plane_copy(part, p, slot):
        sem = part[9]
        return remote(
            part[6].at[p], part[8].at[slot], sem.at[4, p], sem.at[5, slot], index_of(p, x, core)
        )

    for p in others + [plane]:
        for part in parts:
            core_copy(part, p).start()

    def from_core(step, _):
        p = turn(step)
        for part in parts:
            core_copy(part, p).wait_recv()
        for side, out in ((beside, 3), (x, 4)):
            merge(
                [part[1](p, side) for part in parts],
                [part[2].at[p, side] for part in parts],
                [part[out].at[p] for part in parts],
            )
            if out == 3:
                for part in parts:
                    beside_copy(part, p).start()
        return 0

    lax.fori_loop(0, planes, from_core, 0)

    def from_beside(p, outs):
        for part in parts:
            beside_copy(part, p).wait_recv()
        merge([part[4].at[p] for part in parts], [part[5].at[p] for part in parts], outs)

    def to_plane(step, _):
        p = turn(step)
        from_beside(p, [part[6].at[p] for part in parts])
        for part in parts:
            plane_copy(part, p, plane).start()
        return 0

    lax.fori_loop(0, planes - 1, to_plane, 0)
    from_beside(plane, [part[7] for part in parts])
    for p in others:
        for part in parts:
            plane_copy(part, p, p).wait_recv()
    finish([[part[7] for part in parts]] + [[part[8].at[p] for part in parts] for p in others])
    for p in others + [plane]:
        for part in parts:
            core_copy(part, p).wait_send()
            beside_copy(part, p).wait_send()
    for p in others:
        for part in parts:
            plane_copy(part, p, plane).wait_send()


def reduce_scratch(planes, rows, width, dtype):
    return [
        pltpu.VMEM((planes, ROW, rows, width), dtype),
        pltpu.VMEM((planes, rows, width), dtype),
        pltpu.VMEM((planes, rows, width), jnp.float32),
        pltpu.VMEM((planes, rows, width), dtype),
        pltpu.VMEM((planes, rows, width), dtype),
        pltpu.VMEM((rows, width), jnp.float32),
        pltpu.VMEM((planes, rows, width), dtype),
        pltpu.SemaphoreType.DMA((6, planes)),
    ]


STATS = 128


def weigh(stats):
    half = STATS // 2
    tops = [stat[:, :half] for stat in stats]
    top = functools.reduce(jnp.maximum, tops)
    factors = [jnp.exp2(one - top) for one in tops]
    total = sum(stat[:, half:] * factor for stat, factor in zip(stats, factors))
    return top, factors, total


def combine_kernel(n, kept_hbm, sent_ref, stat_ref, cols_ref, *scratch):
    numer_scratch, stat_scratch = scratch[:8], scratch[8:16]
    piece_ref, swap_send, swap_recv, own_sem, kept_ref, kept_sem = scratch[16:]
    keep = pltpu.make_async_copy(kept_hbm, kept_ref, kept_sem)
    keep.start()
    me, plane, x, core = place(n)
    planes = n // (CORES * ROW)
    width = kept_ref.shape[-1]
    heads = width // HEAD_SIZE
    others = [lax.rem(me + step, n) for step in range(1, n)]
    greet(others)
    keep.wait()

    def merge(one, two, out):
        top, factors, total = weigh([one[1][...], two[1][...]])
        out[1][...] = jnp.concatenate([top, total], axis=1)
        for head in range(heads):
            at = slice(head * HEAD_SIZE, (head + 1) * HEAD_SIZE)
            out[0][:, at] = (
                one[0][:, at].astype(jnp.float32) * factors[0][:, head : head + 1]
                + two[0][:, at].astype(jnp.float32) * factors[1][:, head : head + 1]
            ).astype(out[0].dtype)

    def finish(sources):
        _, factors, total = weigh([source[1][...] for source in sources])
        out = []
        for head in range(heads):
            at = slice(head * HEAD_SIZE, (head + 1) * HEAD_SIZE)
            numer = sum(
                source[0][:, at].astype(jnp.float32) * factor[:, head : head + 1]
                for source, factor in zip(sources, factors)
            )
            out.append((numer / total[:, head : head + 1]).astype(jnp.bfloat16))
        attn = jnp.concatenate(out, axis=1)
        share = width // n
        for device in range(n):
            piece_ref[device] = attn[:, device * share : (device + 1) * share]

    reduce_rows(
        (plane, x, core, planes),
        [
            (lambda p: sent_ref.at[p], lambda p, side: kept_ref.at[p, side], *numer_scratch),
            (
                lambda p: stat_ref.at[p, :, 1 - core],
                lambda p, side: stat_ref.at[p, side, core],
                *stat_scratch,
            ),
        ],
        merge,
        finish,
    )

    def swap(device, slot):
        return remote(
            piece_ref.at[device], cols_ref.at[slot], swap_send.at[device], swap_recv.at[slot], device
        )

    own = pltpu.make_async_copy(piece_ref.at[me], cols_ref.at[me], own_sem)
    own.start()
    for device in others:
        swap(device, me).start()
    own.wait()
    for device in others:
        swap(device, device).wait_recv()
    for device in others:
        swap(device, me).wait_send()


def combine(kept, sent, stats, n):
    qtok, width = stats.shape[0], kept.shape[1]
    planes, rows = n // (CORES * ROW), qtok // n
    cols = pl.pallas_call(
        functools.partial(combine_kernel, n),
        out_shape=jax.ShapeDtypeStruct((n, rows, width // n), jnp.bfloat16),
        in_specs=[pl.BlockSpec(memory_space=pl.ANY)] * 2
        + [pl.BlockSpec(memory_space=pltpu.VMEM)],
        out_specs=pl.BlockSpec(memory_space=pltpu.VMEM),
        scratch_shapes=reduce_scratch(planes, rows, width, jnp.bfloat16)
        + reduce_scratch(planes, rows, STATS, jnp.float32)
        + [
            pltpu.VMEM((n, rows, width // n), jnp.bfloat16),
            pltpu.SemaphoreType.DMA((n,)),
            pltpu.SemaphoreType.DMA((n,)),
            pltpu.SemaphoreType.DMA,
            pltpu.VMEM((planes, ROW, rows, width), jnp.float32),
            pltpu.SemaphoreType.DMA,
        ],
        compiler_params=pltpu.CompilerParams(
            collective_id=1, has_side_effects=True, vmem_limit_bytes=60 * 2**20
        ),
        name="combine",
    )(
        kept.reshape(planes, ROW, rows, width),
        sent.reshape(planes, ROW, rows, width),
        stats.reshape(planes, ROW, CORES, rows, STATS),
    )
    return cols.reshape(qtok, width // n)


TILE = 512


def project_kernel(n, cols_ref, weight_hbm, out_ref, weight_ref, weight_sem, kept_ref, sent_ref, *scratch):
    _, plane, x, core = place(n)
    planes = n // (CORES * ROW)
    rows, width = out_ref.shape

    def fetch(tile):
        at = pl.ds(pl.multiple_of(tile * TILE, TILE), TILE)
        return pltpu.make_async_copy(weight_hbm.at[:, at], weight_ref.at[:, at], weight_sem.at[tile])

    for tile in range(width // TILE):
        fetch(tile).start()
    greet(
        [index_of(lax.rem(plane + step, planes), x, core) for step in range(1, planes)]
        + [index_of(plane, 1 - x, core), index_of(plane, x, 1 - core)]
    )

    def tile_step(tile, _):
        at = pl.ds(pl.multiple_of(tile * TILE, TILE), TILE)
        fetch(tile).wait()
        product = jnp.dot(cols_ref[...], weight_ref[:, at], preferred_element_type=jnp.float32)
        product = product.reshape(planes, ROW, CORES, rows, TILE)
        kept_ref[:, :, :, at] = jnp.where(core == 0, product[:, :, 0], product[:, :, 1])
        sent = jnp.where(core == 0, product[:, :, 1], product[:, :, 0])
        sent_ref[:, :, :, at] = sent.astype(sent_ref.dtype)
        return 0

    lax.fori_loop(0, width // TILE, tile_step, 0)

    def merge(one, two, out):
        out[0][...] = (one[0][...].astype(jnp.float32) + two[0][...].astype(jnp.float32)).astype(
            out[0].dtype
        )

    def finish(sources):
        out_ref[...] = sum(source[0][...].astype(jnp.float32) for source in sources).astype(
            out_ref.dtype
        )

    reduce_rows((plane, x, core, planes), [(lambda p: sent_ref.at[p], lambda p, side: kept_ref.at[p, side], *scratch)], merge, finish)


def project(cols, weight, n):
    qtok = cols.shape[0]
    width = weight.shape[1]
    planes, rows = n // (CORES * ROW), qtok // n
    return pl.pallas_call(
        functools.partial(project_kernel, n),
        out_shape=jax.ShapeDtypeStruct((rows, width), jnp.bfloat16),
        in_specs=[pl.BlockSpec(memory_space=pltpu.VMEM), pl.BlockSpec(memory_space=pl.ANY)],
        out_specs=pl.BlockSpec(memory_space=pltpu.VMEM),
        scratch_shapes=[
            pltpu.VMEM(weight.shape, weight.dtype),
            pltpu.SemaphoreType.DMA((width // TILE,)),
        ]
        + [pltpu.VMEM((planes, ROW, rows, width), t) for t in (jnp.float32, jnp.bfloat16)]
        + reduce_scratch(planes, rows, width, jnp.bfloat16),
        compiler_params=pltpu.CompilerParams(
            collective_id=2, has_side_effects=True, vmem_limit_bytes=60 * 2**20
        ),
        name="project",
    )(cols, weight)


def shards_near(n, queries, keys, values, block_mask, out_weight):
    whole = gather_rows(queries, n)
    qtok = whole.shape[0]
    kept, sent, top, total = attend(whole, keys, values, block_mask, queries.shape[0])
    top, total = by_token(top, qtok), by_token(total, qtok)
    room = ((0, 0), (0, STATS // 2 - top.shape[1]))
    stats = jnp.concatenate([jnp.pad(top, room), jnp.pad(total, room)], axis=1)
    cols = combine(kept, sent, stats, n)
    return project(cols, out_weight, n)


def solution(mesh):
    n = mesh.shape["ctx"]

    def shards(queries, *rest):
        fits = n % (CORES * ROW) == 0 and queries.shape[0] == 16
        if fits and queries.shape[1] // HEAD_SIZE <= STATS // 2:
            return shards_near(n, queries, *rest)
        return shards_any(queries, *rest)

    return jax.shard_map(
        shards,
        mesh=mesh,
        in_specs=(
            P(("groups", "ctx"), None),
            P(("groups", "ctx"), None),
            P(("groups", "ctx"), None),
            P("groups", None, "ctx"),
            P("ctx", None),
        ),
        out_specs=P(("groups", "ctx"), None),
        check_vma=False,
    )
```

profile of v0, /device:TPU:0, one launch (start us, length us, event | category | flops | bytes accessed | tf_op | source)
XLA Modules:
  0.0 121.8 jit_solution(3090224837191387254)
XLA Ops:
  0.0 27.3 %gather_rows.1 = bf16[16,16,5120]{2,1,0:T(8,128)(2,1)} custom-call(bf16[16,5120]{1,0:T(8,128)(2,1)} %own_ref.1), custom_call_target="tpu_custom_call" | custom-call | tf_op jit(solution)/shard_map/gather_rows/pallas_call | solution.py:305
  27.3 24.2 %attend.1 = (f32[128,5120]{1,0:T(8,128)}, bf16[128,5120]{1,0:T(8,128)(2,1)}, f32[8,2,640]{2,1,0:T(2,128)}, f32[8,2,640]{2,1,0:T(2,128)}) custom-call(s32[8,2,12]{2,1,0:T(2,128)} %mask_ref.1, bf16[256,5120]{1,0:T(8,128)(2,1)} %bitcast.23, bf16[1536,1024]{1,0:T(8,128)(2,1)} %k_ref.1, bf16[1536,1024]{1,0:T(8,128)(2,1)} %v_ref.1), custom_call_target="tpu_custom_call" | custom-call | tf_op jit(solution)/shard_map/attend/pallas_call | solution.py:119
  51.5 0.8 copy.8
  52.3 0.8 copy.10
  53.2 0.8 copy.12
  54.0 35.0 %combine.1 = bf16[16,16,320]{2,1,0:T(8,128)(2,1)} custom-call(f32[4,2,16,5120]{3,2,1,0:T(8,128)} %bitcast.24, bf16[4,2,16,5120]{3,2,1,0:T(8,128)(2,1)} %bitcast.25, f32[4,2,2,16,128]{4,3,2,1,0:T(8,128)} %bitcast.27), custom_call_target="tpu_custom_call" | custom-call | tf_op jit(solution)/shard_map/combine/pallas_call | solution.py:491
  89.0 31.2 %project.1 = bf16[16,5120]{1,0:T(8,128)(2,1)} custom-call(bf16[256,320]{1,0:T(8,128)(2,1)} %bitcast.26, bf16[320,5120]{1,0:T(8,128)(2,1)} %weight_hbm.1), custom_call_target="tpu_custom_call" | custom-call | tf_op jit(solution)/shard_map/project/pallas_call | solution.py:567
  120.2 1.6 %copy.18 = bf16[16,5120]{1,0:T(8,128)(2,1)} copy(bf16[16,5120]{1,0:T(8,128)(2,1)} %project.1) | data formatting | bytes 327680
  (6 shorter events, 0.1 us)
where the time goes:
time: 122 us
  Pallas kernels  118 us (97%)
  local copies, waits for them, and re-layouts  4.01 us (3%)
    pallas_call x1, Pallas kernels, combine(): pl.pallas_call(functools.partial(combine_kernel, n), out_shape=jax.ShapeD...  35 us
    pallas_call x1, Pallas kernels, project(): pl.pallas_call(functools.partial(project_kernel, n), out_shape=jax.ShapeD...  31.2 us
    pallas_call x1, Pallas kernels, gather_rows(): pl.pallas_call(functools.partial(gather_kernel, n), out_shape=jax.ShapeDt...  27.3 us
    pallas_call x1, Pallas kernels, attend(): pl.pallas_call(functools.partial(attend_kernel, rows_each), grid=(heads_k...  24.2 us

commit v1 on v0

--- a/solution.py
+++ b/solution.py
@@ -516,7 +516,7 @@
     return cols.reshape(qtok, width // n)
 
 
-TILE = 512
+TILE = 1024
 
 
 def project_kernel(n, cols_ref, weight_hbm, out_ref, weight_ref, weight_sem, kept_ref, sent_ref, *scratch):

time: 122 us -> 122 us (level)
    pallas_call x1, Pallas kernels: 35 us -> 39.6 us  [combine(): pl.pallas_call(functools.partial(combine_kernel, n), out_shape=jax.ShapeD...]
    pallas_call x1, Pallas kernels: 24.2 us -> 20.2 us  [attend(): pl.pallas_call(functools.partial(attend_kernel, rows_each), grid=(heads_k...]
where the time goes in v1:
time: 122 us; the launch traced here: 121 us
  Pallas kernels  117 us (96%)
  local copies, waits for them, and re-layouts  4.01 us (3%)
    pallas_call x1, Pallas kernels, combine(): pl.pallas_call(functools.partial(combine_kernel, n), out_shape=jax.ShapeD...  39.6 us
    pallas_call x1, Pallas kernels, project(): pl.pallas_call(functools.partial(project_kernel, n), out_shape=jax.ShapeD...  30.3 us
    pallas_call x1, Pallas kernels, gather_rows(): pl.pallas_call(functools.partial(gather_kernel, n), out_shape=jax.ShapeDt...  27.3 us
    pallas_call x1, Pallas kernels, attend(): pl.pallas_call(functools.partial(attend_kernel, rows_each), grid=(heads_k...  20.2 us

profile of v1, /device:TPU:0, one launch (start us, length us, event | category | flops | bytes accessed | tf_op | source)
XLA Modules:
  0.0 121.5 jit_solution(2816017240924944819)
XLA Ops:
  0.0 27.3 %gather_rows.1 = bf16[16,16,5120]{2,1,0:T(8,128)(2,1)} custom-call(bf16[16,5120]{1,0:T(8,128)(2,1)} %own_ref.1), custom_call_target="tpu_custom_call" | custom-call | tf_op jit(solution)/shard_map/gather_rows/pallas_call | solution.py:305
  27.3 20.2 %attend.1 = (f32[128,5120]{1,0:T(8,128)}, bf16[128,5120]{1,0:T(8,128)(2,1)}, f32[8,2,640]{2,1,0:T(2,128)}, f32[8,2,640]{2,1,0:T(2,128)}) custom-call(s32[8,2,12]{2,1,0:T(2,128)} %mask_ref.1, bf16[256,5120]{1,0:T(8,128)(2,1)} %bitcast.23, bf16[1536,1024]{1,0:T(8,128)(2,1)} %k_ref.1, bf16[1536,1024]{1,0:T(8,128)(2,1)} %v_ref.1), custom_call_target="tpu_custom_call" | custom-call | tf_op jit(solution)/shard_map/attend/pallas_call | solution.py:119
  47.5 0.8 copy.8
  48.4 0.8 copy.10
  49.2 0.8 copy.12
  50.0 39.6 %combine.1 = bf16[16,16,320]{2,1,0:T(8,128)(2,1)} custom-call(f32[4,2,16,5120]{3,2,1,0:T(8,128)} %bitcast.24, bf16[4,2,16,5120]{3,2,1,0:T(8,128)(2,1)} %bitcast.25, f32[4,2,2,16,128]{4,3,2,1,0:T(8,128)} %bitcast.27), custom_call_target="tpu_custom_call" | custom-call | tf_op jit(solution)/shard_map/combine/pallas_call | solution.py:491
  89.6 30.3 %project.1 = bf16[16,5120]{1,0:T(8,128)(2,1)} custom-call(bf16[256,320]{1,0:T(8,128)(2,1)} %bitcast.26, bf16[320,5120]{1,0:T(8,128)(2,1)} %weight_hbm.1), custom_call_target="tpu_custom_call" | custom-call | tf_op jit(solution)/shard_map/project/pallas_call | solution.py:567
  119.9 1.6 %copy.18 = bf16[16,5120]{1,0:T(8,128)(2,1)} copy(bf16[16,5120]{1,0:T(8,128)(2,1)} %project.1) | data formatting | bytes 327680
  (6 shorter events, 0.1 us)
